TPU v7x, 32 devices: a whole 2x2x4 slice. The times are simulated.
32 devices in a mesh: lat: 8 (over z, y), lev: 4 (over x, core).
Axes of the slice: x: 2, y: 2, z: 4, core: 2. Of those that a mesh axis runs over, the one named last changes fastest.
Arguments:
- field: float32 [4, 320, 4096], P(None, 'lat', 'lev'), may hold values from -6 to 6
- weights: bfloat16 [4, 320, 4096], P(None, 'lat', 'lev'), may hold values from 0 to 0.5
- depart_row: int32 [320, 4096], P('lat', 'lev'), may hold values from -2 to 1
- depart_col: int32 [320, 4096], P('lat', 'lev'), may hold values from -2 to 1
- legendre: bfloat16 [320, 16, 640], P('lat'), may hold values from -6 to 6
- wave_slot: int32 [16], replicated, may hold values from 0 to 15, each once
Outputs:
- updated: float32 [4, 320, 4096], P(None, 'lat', 'lev')
- spectral: float32 [16, 2, 4, 2, 640], P('lat', None, 'lev')
Inputs may be any that keep to these rules, and one draw needn't show every extreme that they name: `depart_row`: latitude offsets of departure cells, so that rows i - 2 to i + 2 are read. `depart_col`: longitude offsets of departure cells, so that columns j - 2 to j + 2 are read, periodically. `wave_slot`: A permutation of 0 to 15.
All inputs are finite; a program needn't handle non-finite values.
Results may differ from a plain program's by a relative error of at most 0.0033.
Values may be sent and summed in bfloat16 or wider, within the bound.
A program may use at most 128 MiB of HBM per device.

v0:
```python
import math

import jax
import jax.numpy as jnp
from jax import lax
from jax.sharding import PartitionSpec as P

NLON = 4096
NT = 1279
M_OWN = 2


DAMPING = 4.0


def padded(array, sides, width, wrap):
    for axis, dim in sides:
        size, length = (lax.axis_size(axis), array.shape[dim])
        up = [(i, (i + 1) % size) for i in range(size if wrap else size - 1)]
        down = [(j, i) for i, j in up]
        last = lax.slice_in_dim(array, length - width, length, axis=dim)
        initial = lax.slice_in_dim(array, 0, width, axis=dim)
        before = lax.ppermute(last, axis, up)
        after = lax.ppermute(initial, axis, down)
        array = jnp.concatenate([before, array, after], axis=dim)
    return array


def swapped(value, axis, apart):
    mask = 2**apart
    pairs = [(source, source ^ mask) for source in range(lax.axis_size(axis))]
    return lax.ppermute(value, axis, pairs)


def forward_table(lon_list, wave_list):
    phases = lon_list[:, None] * wave_list[None, :] % NLON
    angles = phases.astype(jnp.float32) * (2.0 * math.pi / NLON)
    return jnp.concatenate([jnp.cos(angles), -jnp.sin(angles)], axis=1) * (1.0 / math.sqrt(NLON))


def inverse_table(wave_list, lon_list, wave_count):
    phases = wave_list[:, None] * lon_list[None, :] % NLON
    angles = phases.astype(jnp.float32) * (2.0 * math.pi / NLON)
    weight = (jnp.where(wave_list == 0, 1.0, 2.0) / math.sqrt(wave_count))[:, None]
    return jnp.concatenate([weight * jnp.cos(angles), -weight * jnp.sin(angles)], axis=0)


def diffuse(raw_sums, slot_waves, steps_count):
    degree = (
        slot_waves[:, None, None]
        + 2 * jnp.arange(steps_count, dtype=jnp.int32)[None, None, :]
        + jnp.arange(2, dtype=jnp.int32)[None, :, None]
    )
    inside = degree <= NT
    factor = 1.0 / (
        1.0 + DAMPING * (degree * (degree + 1)).astype(jnp.float32) / float(NT * (NT + 1))
    )
    masked = jnp.where(inside[:, :, None, None, :], raw_sums, jnp.zeros_like(raw_sums))
    damped = masked * factor[:, :, None, None, :]
    return (damped, (damped - masked).astype(jnp.bfloat16))


def on_device(field, weights, depart_row, depart_col, legendre, wave_slot):
    hp = lax.Precision.HIGHEST
    lat_count = lax.axis_size("lat")
    lev_count = lax.axis_size("lev")
    lat_here = lax.axis_index("lat")
    levels, rows_here, lon_width = field.shape
    lev_local = levels // lev_count
    wave_count = M_OWN * lat_count
    steps_count = legendre.shape[2]
    half_lat = rows_here * lat_count // 2
    northern = lat_here < lat_count // 2
    bit_count = lat_count.bit_length() - 1
    band = padded(field, (("lat", 1),), 2, False)
    padded_block = padded(band, (("lev", 2),), 2, True)
    wide_cols = lon_width + 4
    flattened = padded_block.reshape(levels, (rows_here + 4) * wide_cols)
    row_base = jnp.arange(rows_here, dtype=jnp.int32)[:, None] + 2 + depart_row
    col_base = jnp.arange(lon_width, dtype=jnp.int32)[None, :] + 2 + depart_col
    summed = jnp.zeros((levels, rows_here * lon_width), jnp.float32)
    for row_step in range(2):
        for col_step in range(2):
            source = ((row_base + row_step) * wide_cols + col_base + col_step).reshape(-1)
            corner = weights[2 * row_step + col_step].reshape(-1).astype(jnp.float32)
            summed = summed + corner[None, :] * jnp.take(flattened, source, axis=1)
    advected = summed.reshape(levels, rows_here, lon_width)
    wavenumbers = jnp.arange(wave_count, dtype=jnp.int32) * (NT + 1) // wave_count
    one_hot = (wave_slot[None, :] == jnp.arange(wave_count, dtype=jnp.int32)[:, None]).astype(
        jnp.int32
    )
    k_of_slot = jnp.sum(one_hot * jnp.arange(wave_count, dtype=jnp.int32)[None, :], axis=1)
    slot_waves = jnp.sum(one_hot * wavenumbers[None, :], axis=1)
    columns = lax.all_to_all(advected, "lev", split_axis=0, concat_axis=2, tiled=True)
    wave_table = forward_table(jnp.arange(NLON, dtype=jnp.int32), wavenumbers)
    coeffs = jnp.dot(
        columns.reshape(-1, NLON), wave_table, precision=hp, preferred_element_type=jnp.float32
    )
    fourier = coeffs.reshape(lev_local, rows_here, 2, wave_count).astype(jnp.bfloat16)
    partner = fourier
    for bit_number in range(bit_count):
        partner = swapped(partner, "lat", bit_number)
    partner = jnp.flip(partner, axis=1)
    forward_scale = 1.0 / math.sqrt(half_lat)
    parity = jnp.where(northern, 0, 1).astype(jnp.int32)
    inverse_scale = 1.0 / math.sqrt(steps_count)
    chosen = k_of_slot
    leg_part = jnp.take(legendre, chosen, axis=1)
    own_part = jnp.take(fourier, chosen, axis=3)
    other_part = jnp.take(partner, chosen, axis=3)
    own_term = jnp.einsum("lkj,vlck->kvcj", leg_part, own_part, preferred_element_type=jnp.float32)
    other_term = jnp.einsum(
        "lkj,vlck->kvcj", leg_part, other_part, preferred_element_type=jnp.float32
    )
    combined = jnp.where(northern, own_term + other_term, other_term - own_term) * forward_scale
    nothing = jnp.zeros_like(combined)
    owned_sums = lax.psum_scatter(
        jnp.stack(
            [jnp.where(northern, combined, nothing), jnp.where(northern, nothing, combined)], axis=1
        ),
        "lat",
        scatter_dimension=0,
        tiled=True,
    )
    own_waves = lax.dynamic_slice_in_dim(slot_waves, lat_here * M_OWN, M_OWN, 0)
    damped, change = diffuse(owned_sums, own_waves, steps_count)
    chosen = k_of_slot
    leg_part = jnp.take(legendre, chosen, axis=1)
    own_parity = lax.dynamic_index_in_dim(
        lax.all_gather(change, "lat", axis=0, tiled=True), parity, 1, keepdims=False
    )
    result = jnp.einsum("lkj,kvcj->vlck", leg_part, own_parity, preferred_element_type=jnp.float32)
    half_sum = result * inverse_scale
    across = half_sum
    for bit_number in range(bit_count):
        across = swapped(across, "lat", bit_number)
    across = jnp.flip(across, axis=1)
    synthesis = jnp.where(northern, half_sum + across, across - half_sum)
    synthesis = synthesis.reshape(lev_local, rows_here, 2 * wave_count)
    back_table = inverse_table(slot_waves, jnp.arange(NLON, dtype=jnp.int32), wave_count)
    circles = jnp.dot(
        synthesis.reshape(-1, 2 * wave_count),
        back_table,
        precision=hp,
        preferred_element_type=jnp.float32,
    ).reshape(lev_local, rows_here, NLON)
    increment = lax.all_to_all(circles, "lev", split_axis=2, concat_axis=0, tiled=True)
    updated = advected + increment
    return (updated, damped)


def solution(mesh):
    placed = (
        P(None, "lat", "lev"),
        P(None, "lat", "lev"),
        P("lat", "lev"),
        P("lat", "lev"),
        P("lat", None, None),
        P(),
    )
    return jax.shard_map(
        on_device,
        mesh=mesh,
        in_specs=placed,
        out_specs=(P(None, "lat", "lev"), P("lat", None, "lev", None, None)),
        check_vma=False,
    )
```

profile of v0, /device:TPU:0, one launch (start us, length us, event | category | flops | bytes accessed | tf_op | source)
XLA Modules:
  0.0 875.8 jit_solution(8156510227616605305)
XLA Ops:
  8.3 4.9 collective-permute-start
  19.8 1.9 fusion.29
  25.5 1.7 collective-permute-start.3
  30.1 3.0 gather_fusion.5
  35.9 11.3 %copy.81 = f32[4,45232]{0,1:T(8,128)} copy(f32[4,45232]{1,0:T(4,128)S(1)} %reshape.196) | data formatting | bytes 1447424 | tf_op jit(solution)/shard_map/reshape | solution.py:78
  47.2 142.5 %gather_fusion = f32[40960,4]{1,0:T(8,128)} fusion(f32[4,45232]{0,1:T(8,128)} %copy.81, s32[40960]{0:T(1024)S(1)} %copy-done.4), kind=kCustom, calls=%fused_computation.clone | custom fusion | bytes 1474560 | tf_op jit(solution)/shard_map/jit(_take)/gather | solution.py:86
  189.7 11.4 %copy.82 = f32[40960,4]{0,1:T(4,128)S(1)} copy(f32[40960,4]{1,0:T(8,128)} %gather_fusion) | data formatting | bytes 1310720 | tf_op jit(solution)/shard_map/jit(_take)/gather | solution.py:86
  201.1 142.5 %gather_fusion.1 = f32[40960,4]{1,0:T(8,128)} fusion(f32[4,45232]{0,1:T(8,128)} %copy.81, s32[40960]{0:T(1024)S(1)} %copy-done.5), kind=kCustom, calls=%fused_computation.3.clone | custom fusion | bytes 1474560 | tf_op jit(solution)/shard_map/jit(_take)/gather | solution.py:86
  343.6 11.4 %copy.84 = f32[40960,4]{0,1:T(4,128)S(1)} copy(f32[40960,4]{1,0:T(8,128)} %gather_fusion.1) | data formatting | bytes 1310720 | tf_op jit(solution)/shard_map/jit(_take)/gather | solution.py:86
  355.1 142.5 %gather_fusion.2 = f32[40960,4]{1,0:T(8,128)} fusion(f32[4,45232]{0,1:T(8,128)} %copy.81, s32[40960]{0:T(1024)S(1)} %copy-done.3), kind=kCustom, calls=%fused_computation.4.clone | custom fusion | bytes 1474560 | tf_op jit(solution)/shard_map/jit(_take)/gather | solution.py:86
  497.6 12.2 %copy.86 = f32[40960,4]{0,1:T(4,128)} copy(f32[40960,4]{1,0:T(8,128)} %gather_fusion.2) | data formatting | bytes 1310720 | tf_op jit(solution)/shard_map/jit(_take)/gather | solution.py:86
  509.7 142.5 %gather_fusion.3 = f32[40960,4]{1,0:T(8,128)} fusion(f32[4,45232]{0,1:T(8,128)} %copy.81, s32[40960]{0:T(1024)S(1)} %fusion.28), kind=kCustom, calls=%fused_computation.5.clone | custom fusion | bytes 1474560 | tf_op jit(solution)/shard_map/jit(_take)/gather | solution.py:86
  652.3 12.2 %copy.88 = f32[40960,4]{0,1:T(4,128)} copy(f32[40960,4]{1,0:T(8,128)} %gather_fusion.3) | data formatting | bytes 1310720 | tf_op jit(solution)/shard_map/jit(_take)/gather | solution.py:86
  664.5 2.4 fusion.1
  668.9 3.5 all-to-all-start
  673.9 8.7 all-to-all-done
  684.1 2.7 collective-permute-start.4
  688.5 3.0 collective-permute-start.5
  693.1 3.0 collective-permute-start.6
  702.4 68.8 %all-reduce.3.cloned.1.call-done = f32[16,2,1,2,640]{4,3,0,2,1:T(2,128)} async-done(((f32[16,2,1,2,640]{4,3,0,2,1:T(2,128)}), f32[16,2,1,2,640]{4,3,0,2,1:T(2,128)}) %all-reduce.3.cloned.1.call-update) | async-done | bytes 163856
  771.9 30.6 %all_gather.3 = bf16[16,2,1,2,640]{4,3,0,2,1:T(2,128)(2,1)S(1)} all-gather(bf16[2,2,1,2,640]{4,3,0,2,1:T(2,128)(2,1)S(1)} %get-tuple-element.19), channel_id=1, replica_groups=mesh['lat'=8,'lev'=4] {'lat'}, dimensions={0}, use_global_device_ids=true | all-gather | bytes 92160 | tf_op jit(solution)/shard_map/all_gather | solution.py:130
  803.3 3.3 collective-permute-done.7
  807.3 3.1 collective-permute-done.8
  810.6 1.7 cosine_multiply_fusion
  812.3 2.7 collective-permute-done.9
  815.2 3.4 fusion.9
  819.2 19.4 %reduce = f32[4096,40]{1,0:T(8,128)} reduce(f32[4096,1,40]{2,1,0:T(1,128)S(1)} %bitcast.113, f32[]{:T(128)} %broadcast.351), dimensions={1}, to_apply=%bitcast.100.reduce_sub_computation | reduce | bytes 1310724
  838.6 3.9 reshape.301
  842.5 3.7 all-to-all-start.1
  846.9 9.4 %all-to-all-done.1 = f32[4,1,40960]{2,1,0:T(1,128)S(1)} async-done(((f32[4,1,40960]{2,1,0:T(1,128)}), f32[4,1,40960]{2,1,0:T(1,128)S(1)}, u32[]{:S(2)}, u32[]{:S(2)}) %all-to-all-start.1) | async-done | bytes 655392 | tf_op jit(solution)/shard_map/all_to_all | solution.py:147
  856.2 3.4 reduce.1
  859.6 5.1 reshape.302
  (95 shorter events, 38.9 us)
Async XLA Ops:
  7.2 22.9 %copy-start = (bf16[40,16,640]{2,1,0:T(8,128)(2,1)S(1)}, bf16[40,16,640]{2,1,0:T(8,128)(2,1)}, u32[]{:S(2)}) copy-start(bf16[40,16,640]{2,1,0:T(8,128)(2,1)} %param.16) | copy-start | bytes 2457604
  8.3 15.3 %collective-permute-start = (f32[4,2,1024]{2,1,0:T(2,128)S(1)}, f32[4,2,1024]{2,1,0:T(2,128)S(1)}, u32[]{:S(2)}, u32[]{:S(2)}) collective-permute-start(f32[4,2,1024]{2,1,0:T(2,128)S(1)} %get-tuple-element.23), channel_id=1, source_target_pairs={{0,4},{4,8},{8,12},{12,16},{16,20},{20,24},{24,28},{1,5},{5,9},{9,... | collective-permute-start | bytes 98312 | tf_op jit(solution)/shard_map/ppermute | solution.py:23
  13.2 10.4 %collective-permute-start.1 = (f32[4,2,1024]{2,1,0:T(2,128)S(1)}, f32[4,2,1024]{2,1,0:T(2,128)S(1)}, u32[]{:S(2)}, u32[]{:S(2)}) collective-permute-start(f32[4,2,1024]{2,1,0:T(2,128)S(1)} %get-tuple-element.24), channel_id=1, source_target_pairs={{4,0},{8,4},{12,8},{16,12},{20,16},{24,20},{28,24},{5,1},{9,5},{13... | collective-permute-start | bytes 98312 | tf_op jit(solution)/shard_map/ppermute | solution.py:24
  25.5 7.5 collective-permute-start.2
  25.5 8.2 collective-permute-start.3
  27.3 5.8 copy-start.9
  33.0 14.1 %copy-start.4 = (s32[40960]{0:T(1024)S(1)}, s32[40960]{0:T(1024)}, u32[]{:S(2)}) copy-start(s32[40960]{0:T(1024)} %fusion.25) | copy-start | bytes 491524
  33.1 0.7 copy-start.8
  35.9 165.2 %copy-start.5 = (s32[40960]{0:T(1024)S(1)}, s32[40960]{0:T(1024)}, u32[]{:S(2)}) copy-start(s32[40960]{0:T(1024)} %fusion.26) | copy-start | bytes 491524
  189.7 165.4 %copy-start.3 = (s32[40960]{0:T(1024)S(1)}, s32[40960]{0:T(1024)}, u32[]{:S(2)}) copy-start(s32[40960]{0:T(1024)} %fusion.27) | copy-start | bytes 491524
  497.6 166.9 %copy-start.6 = (f32[5,8,8,128]{3,1,2,0:T(8,128)S(1)}, f32[5,8,8,128]{3,1,2,0:T(8,128)}, u32[]{:S(2)}) copy-start(f32[5,8,8,128]{3,1,2,0:T(8,128)} %copy.104) | copy-start | bytes 491524
  497.6 166.9 %copy-start.7 = (f32[5,8,8,128]{3,1,2,0:T(8,128)S(1)}, f32[5,8,8,128]{3,1,2,0:T(8,128)}, u32[]{:S(2)}) copy-start(f32[5,8,8,128]{3,1,2,0:T(8,128)} %copy.106) | copy-start | bytes 491524
  509.7 162.9 %copy-start.10 = (pred[16]{0:T(512)(128)(4,1)S(1)}, pred[16]{0:T(512)(128)(4,1)}, u32[]{:S(2)}) copy-start(pred[16]{0:T(512)(128)(4,1)} %compare_and_fusion.4) | copy-start | bytes 52
  652.2 216.7 %copy-start.1 = (bf16[40,16,640]{2,1,0:T(8,128)(2,1)S(1)}, bf16[40,16,640]{2,1,0:T(8,128)(2,1)}, u32[]{:S(2)}) copy-start(bf16[40,16,640]{2,1,0:T(8,128)(2,1)} %param.16) | copy-start | bytes 2457604
  666.8 0.8 copy-start.2
  668.9 13.7 %all-to-all-start = ((f32[4,40,1024]{2,1,0:T(8,128)}), f32[4,40,1024]{2,1,0:T(8,128)S(1)}, u32[]{:S(2)}, u32[]{:S(2)}) async-start(f32[4,40,1024]{2,1,0:T(8,128)} %bitcast.109), calls=%async_computation | async-start | bytes 1310720 | tf_op jit(solution)/shard_map/all_to_all | solution.py:94
  672.4 98.8 %all-reduce.3.cloned.1.call-start = ((), (), s32[]{:S(2)}) async-start(), calls=%async_computation.2 | async-start | bytes 327680
  684.1 4.3 collective-permute-start.4
  688.5 4.6 collective-permute-start.5
  693.1 5.8 collective-permute-start.6
  802.9 3.8 collective-permute-start.7
  806.6 3.7 collective-permute-start.8
  810.4 4.6 collective-permute-start.9
  842.5 13.7 %all-to-all-start.1 = ((f32[4,1,40960]{2,1,0:T(1,128)}), f32[4,1,40960]{2,1,0:T(1,128)S(1)}, u32[]{:S(2)}, u32[]{:S(2)}) async-start(f32[4,1,40960]{2,1,0:T(1,128)} %reshape.301), calls=%async_computation.1 | async-start | bytes 1310720 | tf_op jit(solution)/shard_map/all_to_all | solution.py:147
Sparse Core Ops, SparseCore 0:
  702.5 68.6 all-reduce.2
where the time goes:
time: 877 us; the launch traced here: 876 us
  local copies, waits for them, and re-layouts  659 us (75%)
  waiting for transfers between devices  98.5 us (11%)
  other arithmetic  42 us (5%)
  blocking collectives  30.6 us (3%)
  starting transfers between devices  24.7 us (3%)
  between operations  15.1 us (2%)
    gather x8, local copies, waits for them, and re-layouts, on_device(): summed = summed + corner[None, :] * jnp.take(flattened, source, axis=1)  617 us
    unnamed x2, waiting for transfers between devices  68.8 us
    all_gather x1, blocking collectives, on_device(): lax.all_gather(change, 'lat', axis=0, tiled=True)  30.6 us
    unnamed x3, other arithmetic  21.6 us
    unnamed x37, local copies, waits for them, and re-layouts  18.4 us
  transfers between devices with their start and end apart: 13, of which 8 were waited for; matrix products, arithmetic and copies ran while one was open for 2% of the time, Pallas kernels for 0%

commit v1 on v0

v1 whole, which is shorter than its diff:
```python
import functools
import math

import jax
import jax.numpy as jnp
import numpy as np
from jax import lax
from jax.experimental import pallas as pl
from jax.experimental.pallas import tpu as pltpu
from jax.sharding import PartitionSpec as P

NLON = 4096
NT = 1279
DAMPING = 4.0
LANES = 128
HALF = 64
MESH = pl.DeviceIdType.MESH
F32 = jnp.float32
BF16 = jnp.bfloat16


def lon_table(waves):
    m = (np.arange(waves, dtype=np.int64) * (NT + 1)) // waves
    phases = (m[:, None] * np.arange(NLON, dtype=np.int64)[None, :]) % NLON
    angles = phases.astype(np.float64) * (2.0 * math.pi / NLON)
    table = np.concatenate([np.cos(angles), -np.sin(angles)], axis=0) / math.sqrt(NLON)
    table = table.astype(np.float32)
    lead = table.astype(BF16)
    rest = (table - lead.astype(np.float32)).astype(BF16)
    return np.concatenate([lead, rest], axis=0)


def kernel(
    n_lat, n_lev,
    slot_ref, field_hbm, weights_hbm, drow_hbm, dcol_hbm, leg_hbm, table_hbm,
    out_ref, spec_ref,
    ext, shifted, wts, drow, dcol, leg, tab, adv, inv,
    pack_row, pack_col, got_row, got_col, got_corner,
    send_f, got_f, send_x, got_x, sums, send_s, got_s, send_c, got_c,
    chg_slot, chg, send_h, got_h,
    load_sem, halo_send, halo_recv, f_send, f_recv, x_send, x_recv,
    s_send, s_recv, c_send, c_recv, h_send, h_recv,
):
    levels, rows, width = out_ref.shape
    tiles = width // LANES
    waves, steps = leg.shape[1], leg.shape[2]
    l, e = lax.axis_index("lat"), lax.axis_index("lev")
    mirror = n_lat - 1 - l
    has_up, has_down = l > 0, l < n_lat - 1
    east, west = lax.rem(e + 1, n_lev), lax.rem(e + n_lev - 1, n_lev)
    others = lambda start, size: [lax.rem(start + off, size) for off in range(1, size)]

    loads = []

    def load(src, dst):
        copy = pltpu.make_async_copy(src, dst, load_sem.at[len(loads)])
        copy.start()
        loads.append(copy)

    for t in range(tiles):
        load(
            field_hbm.at[:, :, pl.ds(t * LANES, LANES)],
            ext.at[:, t + 1, pl.ds(8, rows), :],
        )
    load(weights_hbm, wts)
    load(drow_hbm, drow)
    load(dcol_hbm, dcol)
    load(table_hbm.at[:, pl.ds(pl.multiple_of(e * width, LANES), width)], tab)
    load(leg_hbm, leg)

    barrier = pltpu.get_barrier_semaphore()

    def greet(lat, lev):
        pl.semaphore_signal(barrier, inc=1, device_id=(lat, lev), device_id_type=MESH)

    for d in others(l, n_lat):
        greet(d, e)
    for d in others(e, n_lev):
        greet(l, d)
        greet(mirror, d)

    @pl.when(has_up)
    def _():
        greet(l - 1, east)
        greet(l - 1, west)

    @pl.when(has_down)
    def _():
        greet(l + 1, east)
        greet(l + 1, west)

    def find(s, carry):
        def step(k, found):
            return jnp.where(slot_ref[k] == s, k, found)

        inv[s] = lax.fori_loop(0, waves, step, jnp.int32(0))
        return carry

    lax.fori_loop(0, waves, find, 0)

    lane = lax.broadcasted_iota(jnp.int32, (rows, LANES), 1)
    for t in range(tiles):
        loads[t].wait()
    for v in range(levels):
        for t in range(tiles):
            cols = slice(t * LANES, (t + 1) * LANES)
            pack_row[0, 2 * v : 2 * v + 2, cols] = ext[v, t + 1, 6 + rows : 8 + rows, :]
            pack_row[1, 2 * v : 2 * v + 2, cols] = ext[v, t + 1, 8:10, :]
    last = jnp.zeros((rows, LANES), F32)
    first = jnp.zeros((rows, LANES), F32)
    for v in range(levels):
        here = (lane == 2 * v) | (lane == 2 * v + 1)
        tail = pltpu.roll(ext[v, tiles, 8 : 8 + rows, :], (2 * v + 2) % LANES, 1)
        last = jnp.where(here, tail, last)
        head = ext[v, 1, 8 : 8 + rows, :]
        if v:
            head = pltpu.roll(head, 2 * v, 1)
        first = jnp.where(here, head, first)
    pack_col[0] = last
    pack_col[1] = first

    n_greet = (n_lat - 1) + 2 * (n_lev - 1)
    n_greet = n_greet + jnp.where(has_up, 2, 0) + jnp.where(has_down, 2, 0)
    pl.semaphore_wait(barrier, n_greet)

    def remote(src, dst, ssem, rsem, lat, lev):
        return pltpu.make_async_remote_copy(
            src_ref=src, dst_ref=dst, send_sem=ssem, recv_sem=rsem,
            device_id=(lat, lev), device_id_type=MESH,
        )

    def halo(n, src, dst, lat, lev):
        return remote(src, dst, halo_send.at[n], halo_recv.at[n], lat, lev)

    bottom, top = pl.ds(rows - 8, 8), pl.ds(0, 8)
    flat = [
        halo(0, pack_col.at[0], got_col.at[0], l, east),
        halo(1, pack_col.at[1], got_col.at[1], l, west),
    ]
    below = [
        halo(2, pack_row.at[0], got_row.at[0], l + 1, e),
        halo(3, pack_col.at[0, bottom], got_corner.at[0], l + 1, east),
        halo(4, pack_col.at[1, bottom], got_corner.at[1], l + 1, west),
    ]
    above = [
        halo(5, pack_row.at[1], got_row.at[1], l - 1, e),
        halo(6, pack_col.at[0, top], got_corner.at[2], l - 1, east),
        halo(7, pack_col.at[1, top], got_corner.at[3], l - 1, west),
    ]

    @pl.when(has_down)
    def _():
        for copy in below:
            copy.start()

    @pl.when(has_up)
    def _():
        for copy in above:
            copy.start()

    for copy in flat:
        copy.start()

    def spread(piece, v):
        return pltpu.roll(piece, LANES - 2 - 2 * v, 1)

    def spread_east(piece, v):
        return pltpu.roll(piece, LANES - 2 * v, 1) if v else piece

    def rim(row0, size, from_west, from_east):
        for v in range(levels):
            ext[v, 0, row0 : row0 + size, :] = spread(from_west, v)
            ext[v, tiles + 1, row0 : row0 + size, :] = spread_east(from_east, v)

    def fill_rows(which, row0):
        for v in range(levels):
            for t in range(tiles):
                cols = slice(t * LANES, (t + 1) * LANES)
                ext[v, t + 1, row0 : row0 + 2, :] = got_row[which, 2 * v : 2 * v + 2, cols]

    @pl.when(has_up)
    def _():
        for copy in below:
            copy.wait_recv()
        fill_rows(0, 6)
        rim(0, 8, got_corner[0], got_corner[1])

    @pl.when(jnp.logical_not(has_up))
    def _():
        ext[:, :, 0:8, :] = jnp.zeros((levels, tiles + 2, 8, LANES), F32)

    @pl.when(has_down)
    def _():
        for copy in above:
            copy.wait_recv()
        fill_rows(1, rows + 8)
        rim(rows + 8, 8, got_corner[2], got_corner[3])

    @pl.when(jnp.logical_not(has_down))
    def _():
        ext[:, :, rows + 8 : rows + 16, :] = jnp.zeros((levels, tiles + 2, 8, LANES), F32)

    for copy in flat:
        copy.wait_recv()
    rim(8, rows, got_col[0], got_col[1])

    tall = rows + 16
    tall_lane = lax.broadcasted_iota(jnp.int32, (tall, LANES), 1)

    def shift_tile(n, carry):
        v, t = n // tiles, n % tiles
        left, here, right = ext[v, t], ext[v, t + 1], ext[v, t + 2]
        for n_move, move in enumerate((-2, -1, 1, 2)):
            amount = (-move) % LANES
            mine = pltpu.roll(here, amount, 1)
            if move < 0:
                moved = jnp.where(tall_lane < -move, pltpu.roll(left, amount, 1), mine)
            else:
                moved = jnp.where(tall_lane >= LANES - move, pltpu.roll(right, amount, 1), mine)
            shifted[n_move, v, t] = moved
        return carry

    lax.fori_loop(0, levels * tiles, shift_tile, 0)

    for n in range(tiles, tiles + 3):
        loads[n].wait()

    def advect_tile(t, carry):
        cols = pl.ds(pl.multiple_of(t * LANES, LANES), LANES)
        corner = [wts[ab, :, cols].astype(F32) for ab in range(4)]
        for g in range(rows // 8):
            band = slice(8 * g, 8 * g + 8)
            dr, dc = drow[band, cols], dcol[band, cols]
            zero = jnp.zeros((8, LANES), F32)
            in_col = {c: dc == c for c in range(-2, 2)}
            in_row = {r: dr == r for r in range(-2, 2)}

            def pick(masks, at, one, two):
                value = zero
                if at - 1 in masks:
                    value = jnp.where(masks[at - 1], two, value)
                if at in masks:
                    value = jnp.where(masks[at], one, value)
                return value

            part = [
                [pick(in_col, c, corner[2 * a][band], corner[2 * a + 1][band]) for c in range(-2, 3)]
                for a in range(2)
            ]
            coef = [
                [pick(in_row, r, part[0][c], part[1][c]) for c in range(5)] for r in range(-2, 3)
            ]
            for v in range(levels):
                total = None
                for r in range(5):
                    at = pl.ds(8 * g + 6 + r, 8)
                    for c in range(5):
                        if c == 2:
                            value = ext[v, t + 1, at, :]
                        else:
                            value = shifted[c if c < 2 else c - 1, v, t, at, :]
                        term = coef[r][c] * value
                        total = term if total is None else total + term
                adv[v * rows + 8 * g : v * rows + 8 * g + 8, cols] = total
        return carry

    lax.fori_loop(0, tiles, advect_tile, 0)

    loads[tiles + 3].wait()
    contract_last = (((1,), (1,)), ((), ()))
    send_f[...] = jnp.zeros_like(send_f)
    for v in range(levels):
        value = adv[v * rows : (v + 1) * rows, :]
        lead = value.astype(BF16)
        rest = (value - lead.astype(F32)).astype(BF16)
        both = lax.dot_general(tab[...], lead, contract_last, preferred_element_type=F32)
        more = lax.dot_general(
            tab[0 : 2 * waves, :], rest, contract_last, preferred_element_type=F32
        )
        coeffs = both[0 : 2 * waves] + both[2 * waves :] + more
        send_f[v, :, 0:rows] = coeffs[0:waves]
        send_f[v, :, HALF : HALF + rows] = coeffs[waves:]
    copies_f = []
    for d in others(e, n_lev):
        copy = remote(send_f.at[d], got_f.at[e], f_send.at[d], f_recv.at[e], l, d)
        copy.start()
        copies_f.append(copy)
    got_f[e] = send_f[e]
    for d in others(e, n_lev):
        remote(send_f.at[d], got_f.at[d], f_send.at[d], f_recv.at[d], l, d).wait_recv()
    total = got_f[0]
    for d in range(1, n_lev):
        total = total + got_f[d]
    fourier = total.astype(BF16)
    send_x[...] = fourier
    copy_x = remote(send_x, got_x, x_send, x_recv, mirror, e)
    copy_x.start()

    at_row = lax.broadcasted_iota(jnp.int32, (LANES, LANES), 0)
    at_col = lax.broadcasted_iota(jnp.int32, (LANES, LANES), 1)
    flip = ((at_row + at_col == rows - 1) & (at_row < HALF) & (at_col < HALF)) | (
        (at_row + at_col == 2 * HALF + rows - 1) & (at_row >= HALF) & (at_col >= HALF)
    )
    flip = flip.astype(F32)
    sign = jnp.where(l < n_lat // 2, 1.0, -1.0).astype(F32)
    loads[tiles + 4].wait()
    copy_x.wait_recv()
    partner = jnp.dot(got_x[...], flip.astype(BF16), preferred_element_type=F32)
    combined = partner + sign * fourier.astype(F32)

    forward_scale = 1.0 / math.sqrt(rows * n_lat // 2)
    group = 16
    for k0 in range(0, waves, group):
        ks = slice(k0, k0 + group)
        real = jnp.zeros((group, steps), F32)
        imag = jnp.zeros((group, steps), F32)
        for i in range(rows):
            values = leg[i, ks, :].astype(F32)
            real = real + values * combined[ks, i : i + 1]
            imag = imag + values * combined[ks, HALF + i : HALF + i + 1]
        sums[0, ks, :] = real * forward_scale
        sums[1, ks, :] = imag * forward_scale
    for s in range(waves):
        k = inv[s]
        send_s[s, 0:1, :] = sums[0, pl.ds(k, 1), :]
        send_s[s, 1:2, :] = sums[1, pl.ds(k, 1), :]
    own = waves // n_lat
    copies_s = []
    for d in others(l, n_lat):
        copy = remote(
            send_s.at[pl.ds(d * own, own)], got_s.at[l], s_send.at[d], s_recv.at[l], d, e
        )
        copy.start()
        copies_s.append(copy)
    got_s[l] = send_s[pl.ds(l * own, own)]
    for d in others(l, n_lat):
        remote(
            send_s.at[pl.ds(d * own, own)], got_s.at[d], s_send.at[d], s_recv.at[d], d, e
        ).wait_recv()

    column = lax.broadcasted_iota(jnp.int32, (2, steps), 1)
    for p in range(2):
        start = p * (n_lat // 2)
        raw = got_s[start]
        for d in range(start + 1, start + n_lat // 2):
            raw = raw + got_s[d]
        for so in range(own):
            wave = inv[l * own + so] * (NT + 1) // waves
            degree = wave + 2 * column + p
            factor = 1.0 / (
                1.0 + DAMPING * (degree * (degree + 1)).astype(F32) / float(NT * (NT + 1))
            )
            masked = jnp.where(degree <= NT, raw[so], 0.0)
            damped = masked * factor
            spec_ref[so, p, 0] = damped
            send_c[p, so] = (damped - masked).astype(BF16)
    copies_c = []
    parity_of = lambda d: d // (n_lat // 2)
    for d in others(l, n_lat):
        copy = remote(send_c.at[parity_of(d)], got_c.at[l], c_send.at[d], c_recv.at[l], d, e)
        copy.start()
        copies_c.append(copy)
    got_c[l] = send_c[parity_of(l)]
    for d in others(l, n_lat):
        remote(
            send_c.at[parity_of(d)], got_c.at[d], c_send.at[d], c_recv.at[d], d, e
        ).wait_recv()

    for d in range(n_lat):
        for so in range(own):
            chg_slot[d * own + so] = got_c[d, so].astype(F32)
    for k in range(waves):
        value = chg_slot[slot_ref[k]]
        chg[0, k : k + 1, :] = value[0:1]
        chg[1, k : k + 1, :] = value[1:2]
    inverse_scale = math.sqrt(NLON) / math.sqrt(waves) / math.sqrt(steps)
    lane = lax.broadcasted_iota(jnp.int32, (group, LANES), 1)
    wave_row = lax.broadcasted_iota(jnp.int32, (group, LANES), 0)
    for k0 in range(0, waves, group):
        ks = slice(k0, k0 + group)
        real, imag = chg[0, ks, :], chg[1, ks, :]
        half = jnp.zeros((group, LANES), F32)
        for i in range(rows):
            values = leg[i, ks, :].astype(F32)
            half = jnp.where(lane == i, jnp.sum(values * real, axis=1, keepdims=True), half)
            half = jnp.where(
                lane == HALF + i, jnp.sum(values * imag, axis=1, keepdims=True), half
            )
        half = half * jnp.where(wave_row + k0 == 0, inverse_scale, 2.0 * inverse_scale)
        send_h[0, ks, :] = half
        send_h[1, ks, :] = jnp.dot(
            half, flip, precision=lax.Precision.HIGHEST, preferred_element_type=F32
        )
    copies_h = []
    for off in range(n_lev):
        d = lax.rem(e + off, n_lev)
        copy = remote(send_h.at[1], got_h.at[1, e], h_send.at[1, d], h_recv.at[1, e], mirror, d)
        copy.start()
        copies_h.append(copy)
    for d in others(e, n_lev):
        copy = remote(send_h.at[0], got_h.at[0, e], h_send.at[0, d], h_recv.at[0, e], l, d)
        copy.start()
        copies_h.append(copy)
    got_h[0, e] = send_h[0]
    for d in others(e, n_lev):
        remote(
            send_h.at[0], got_h.at[0, d], h_send.at[0, d], h_recv.at[0, d], l, d
        ).wait_recv()
    for off in range(n_lev):
        d = lax.rem(e + off, n_lev)
        remote(
            send_h.at[1], got_h.at[1, d], h_send.at[1, d], h_recv.at[1, d], mirror, d
        ).wait_recv()

    stack = []
    for v in range(levels):
        synthesis = got_h[1, v] + sign * got_h[0, v]
        both = jnp.concatenate([synthesis, pltpu.roll(synthesis, HALF, 1)], axis=0)
        stack.append(jnp.transpose(both)[0:rows, :])
    synthesis = jnp.concatenate(stack, axis=0)
    lead = synthesis.astype(BF16)
    rest = (synthesis - lead.astype(F32)).astype(BF16)
    chunk = min(width, 256)
    for j in range(0, width, chunk):
        cols = slice(j, j + chunk)
        table, table_rest = tab[0 : 2 * waves, cols], tab[2 * waves :, cols]
        increment = (
            jnp.dot(lead, table, preferred_element_type=F32)
            + jnp.dot(lead, table_rest, preferred_element_type=F32)
            + jnp.dot(rest, table, preferred_element_type=F32)
        )
        updated = adv[:, cols] + increment
        for v in range(levels):
            out_ref[v, :, cols] = updated[v * rows : (v + 1) * rows]

    for copy in flat + copies_f + [copy_x] + copies_s + copies_c + copies_h:
        copy.wait_send()

    @pl.when(has_down)
    def _():
        for copy in below:
            copy.wait_send()

    @pl.when(has_up)
    def _():
        for copy in above:
            copy.wait_send()


def solution(mesh):
    n_lat, n_lev = mesh.shape["lat"], mesh.shape["lev"]

    def on_device(field, weights, depart_row, depart_col, legendre, wave_slot):
        levels, rows, width = field.shape
        _, waves, steps = legendre.shape
        tiles = width // LANES
        own = waves // n_lat
        table = jnp.asarray(lon_table(waves))
        vmem, dma = pltpu.VMEM, pltpu.SemaphoreType.DMA
        anywhere = pl.BlockSpec(memory_space=pl.ANY)
        in_vmem = pl.BlockSpec(memory_space=pltpu.VMEM)
        return pl.pallas_call(
            functools.partial(kernel, n_lat, n_lev),
            out_shape=(
                jax.ShapeDtypeStruct((levels, rows, width), F32),
                jax.ShapeDtypeStruct((own, 2, 1, 2, steps), F32),
            ),
            in_specs=[pl.BlockSpec(memory_space=pltpu.SMEM)] + [anywhere] * 6,
            out_specs=(in_vmem, in_vmem),
            scratch_shapes=[
                vmem((levels, tiles + 2, rows + 16, LANES), F32),
                vmem((4, levels, tiles, rows + 16, LANES), F32),
                vmem((4, rows, width), BF16),
                vmem((rows, width), jnp.int32),
                vmem((rows, width), jnp.int32),
                vmem((rows, waves, steps), BF16),
                vmem((4 * waves, width), BF16),
                vmem((levels * rows, width), F32),
                pltpu.SMEM((waves,), jnp.int32),
                vmem((2, 2 * levels, width), F32),
                vmem((2, rows, LANES), F32),
                vmem((2, 2 * levels, width), F32),
                vmem((2, rows, LANES), F32),
                vmem((4, 8, LANES), F32),
                vmem((n_lev, waves, LANES), F32),
                vmem((n_lev, waves, LANES), F32),
                vmem((waves, LANES), BF16),
                vmem((waves, LANES), BF16),
                vmem((2, waves, steps), F32),
                vmem((waves, 2, steps), F32),
                vmem((n_lat, own, 2, steps), F32),
                vmem((2, own, 2, steps), BF16),
                vmem((n_lat, own, 2, steps), BF16),
                vmem((waves, 2, steps), F32),
                vmem((2, waves, steps), F32),
                vmem((2, waves, LANES), F32),
                vmem((2, n_lev, waves, LANES), F32),
                dma((tiles + 5,)),
                dma((8,)), dma((8,)),
                dma((n_lev,)), dma((n_lev,)),
                dma, dma,
                dma((n_lat,)), dma((n_lat,)),
                dma((n_lat,)), dma((n_lat,)),
                dma((2, n_lev)), dma((2, n_lev)),
            ],
            compiler_params=pltpu.CompilerParams(
                collective_id=0, has_side_effects=True, vmem_limit_bytes=48 << 20
            ),
        )(wave_slot, field, weights, depart_row, depart_col, legendre, table)

    placed = (
        P(None, "lat", "lev"),
        P(None, "lat", "lev"),
        P("lat", "lev"),
        P("lat", "lev"),
        P("lat", None, None),
        P(),
    )
    return jax.shard_map(
        on_device,
        mesh=mesh,
        in_specs=placed,
        out_specs=(P(None, "lat", "lev"), P("lat", None, "lev", None, None)),
        check_vma=False,
    )
```

time: 877 us -> 48.7 us (0.06)
  local copies, waits for them, and re-layouts: 659 us -> 8.17 us
  waiting for transfers between devices: 98.5 us -> 0 us
  other arithmetic: 42 us -> 0 us
  Pallas kernels: 0 us -> 39.6 us
  blocking collectives: 30.6 us -> 0 us
  starting transfers between devices: 24.7 us -> 0 us
  between operations: 15.1 us -> 0.65 us
    gather x11 -> x0, local copies, waits for them, and re-layouts: 622 us -> none  [the longest x8 617 us: on_device(): summed = summed + corner[None, :] * jnp.take(flattened, source, axis=1)]
    unnamed x2 -> x0, waiting for transfers between devices: 68.8 us -> none
    pallas_call x0 -> x1, Pallas kernels: none -> 39.6 us  [on_device(): pl.pallas_call(functools.partial(kernel, n_lat, n_lev), out_shape=(jax.Sh...]
    all_gather x1 -> x0, blocking collectives: 30.6 us -> none  [on_device(): lax.all_gather(change, 'lat', axis=0, tiled=True)]
    unnamed x3 -> x0, other arithmetic: 21.6 us -> none
    all_to_all x2 -> x0, waiting for transfers between devices: 18.1 us -> none  [the longest x1 9.35 us: on_device(): lax.all_to_all(circles, 'lev', split_axis=2, concat_axis=0, tiled=True)]
    ppermute x10 -> x0, starting transfers between devices: 17.3 us -> none  [the longest x6 9.35 us: swapped(): return lax.ppermute(value, axis, pairs)]
    reshape x3 -> x0, local copies, waits for them, and re-layouts: 12.5 us -> none  [the longest x2 12 us: on_device(): flattened = padded_block.reshape(levels, (rows_here + 4) * wide_cols)]
  transfers between devices with their start and end apart: 13 -> 0, of which waited for: 8 -> 0; matrix products, arithmetic and copies ran while one was open for 2% -> 0% of each run, Pallas kernels for 0% -> 0%
where the time goes in v1:
time: 48.7 us; the launch traced here: 48.4 us
  Pallas kernels  39.6 us (81%)
  local copies, waits for them, and re-layouts  8.17 us (17%)
  between operations  0.65 us (1%)
    pallas_call x1, Pallas kernels, on_device(): pl.pallas_call(functools.partial(kernel, n_lat, n_lev), out_shape=(jax.Sh...  39.6 us
    unnamed x16, local copies, waits for them, and re-layouts  8.17 us

profile of v1, /device:TPU:0, one launch (start us, length us, event | category | flops | bytes accessed | tf_op | source)
XLA Modules:
  0.0 48.4 jit_solution(4012884450908339061)
XLA Ops:
  0.6 0.0 copy-start
  0.6 1.1 %copy-done = bf16[40,16,640]{2,1,0:T(8,128)(2,1)S(1)} copy-done((bf16[40,16,640]{2,1,0:T(8,128)(2,1)S(1)}, bf16[40,16,640]{2,1,0:T(8,128)(2,1)}, u32[]{:S(2)}) %copy-start) | copy-done | bytes 819224
  1.8 0.0 copy-start.1
  1.8 1.1 %copy-done.1 = f32[4,40,1024]{2,1,0:T(8,128)S(1)} copy-done((f32[4,40,1024]{2,1,0:T(8,128)S(1)}, f32[4,40,1024]{2,1,0:T(8,128)}, u32[]{:S(2)}) %copy-start.1) | copy-done | bytes 655384
  2.9 0.0 copy-start.2
  2.9 1.0 %copy-done.2 = bf16[64,4096]{1,0:T(8,128)(2,1)S(1)} copy-done((bf16[64,4096]{1,0:T(8,128)(2,1)S(1)}, bf16[64,4096]{1,0:T(8,128)(2,1)}, u32[]{:S(2)}) %copy-start.2) | copy-done | bytes 524312
  3.9 0.0 copy-start.3
  3.9 1.0 %copy-done.3 = bf16[4,40,1024]{2,1,0:T(8,128)(2,1)S(1)} copy-done((bf16[4,40,1024]{2,1,0:T(8,128)(2,1)S(1)}, bf16[4,40,1024]{2,1,0:T(8,128)(2,1)}, u32[]{:S(2)}) %copy-start.3) | copy-done | bytes 327704
  4.9 0.0 copy-start.4
  4.9 0.9 %copy-done.4 = s32[40,1024]{1,0:T(8,128)S(1)} copy-done((s32[40,1024]{1,0:T(8,128)S(1)}, s32[40,1024]{1,0:T(8,128)}, u32[]{:S(2)}) %copy-start.4) | copy-done | bytes 163864
  5.8 0.0 copy-start.5
  5.8 0.9 %copy-done.5 = s32[40,1024]{1,0:T(8,128)S(1)} copy-done((s32[40,1024]{1,0:T(8,128)S(1)}, s32[40,1024]{1,0:T(8,128)}, u32[]{:S(2)}) %copy-start.5) | copy-done | bytes 163864
  6.7 0.0 copy-start.6
  6.7 0.7 %copy-done.6 = s32[16]{0:T(128)S(1)} copy-done((s32[16]{0:T(128)S(1)}, s32[16]{0:T(128)}, u32[]{:S(2)}) %copy-start.6) | copy-done | bytes 88
  7.4 39.6 %shard_map.86 = (f32[4,40,1024]{2,1,0:T(8,128)S(1)}, f32[2,2,1,2,640]{4,3,2,1,0:T(2,128)S(1)}) custom-call(s32[16]{0:T(128)S(1)} %copy-done.6, f32[4,40,1024]{2,1,0:T(8,128)S(1)} %copy-done.1, bf16[4,40,1024]{2,1,0:T(8,128)(2,1)S(1)} %copy-done.3, s32[40,1024]{1,0:T(8,128)S(1)} %copy-done.4, s32[40,1024]{1,0:T(8,128)S(1)} %copy-done.5, ...), custom_call_target="tpu_custom_call" | custom-call | tf_op jit(solution)/shard_map/pallas_call | solution.py:462
  46.9 0.8 %copy.11 = f32[4,40,1024]{2,1,0:T(8,128)} copy(f32[4,40,1024]{2,1,0:T(8,128)S(1)} %get-tuple-element.4) | data formatting | bytes 1310720
  47.8 0.6 %copy.12 = f32[2,2,1,2,640]{4,3,2,1,0:T(2,128)} copy(f32[2,2,1,2,640]{4,3,2,1,0:T(2,128)S(1)} %get-tuple-element.5) | data formatting | bytes 40960
Async XLA Ops:
  0.6 1.1 %copy-start = (bf16[40,16,640]{2,1,0:T(8,128)(2,1)S(1)}, bf16[40,16,640]{2,1,0:T(8,128)(2,1)}, u32[]{:S(2)}) copy-start(bf16[40,16,640]{2,1,0:T(8,128)(2,1)} %leg_hbm.1) | copy-start | bytes 2457604
  1.8 1.1 %copy-start.1 = (f32[4,40,1024]{2,1,0:T(8,128)S(1)}, f32[4,40,1024]{2,1,0:T(8,128)}, u32[]{:S(2)}) copy-start(f32[4,40,1024]{2,1,0:T(8,128)} %field_hbm.1) | copy-start | bytes 1966084
  2.9 1.0 %copy-start.2 = (bf16[64,4096]{1,0:T(8,128)(2,1)S(1)}, bf16[64,4096]{1,0:T(8,128)(2,1)}, u32[]{:S(2)}) copy-start(bf16[64,4096]{1,0:T(8,128)(2,1)} %constant.2.clone.table_hbm) | copy-start | bytes 1572868
  3.9 1.0 %copy-start.3 = (bf16[4,40,1024]{2,1,0:T(8,128)(2,1)S(1)}, bf16[4,40,1024]{2,1,0:T(8,128)(2,1)}, u32[]{:S(2)}) copy-start(bf16[4,40,1024]{2,1,0:T(8,128)(2,1)} %weights_hbm.1) | copy-start | bytes 983044
  4.9 0.9 %copy-start.4 = (s32[40,1024]{1,0:T(8,128)S(1)}, s32[40,1024]{1,0:T(8,128)}, u32[]{:S(2)}) copy-start(s32[40,1024]{1,0:T(8,128)} %drow_hbm.1) | copy-start | bytes 491524
  5.8 0.9 %copy-start.5 = (s32[40,1024]{1,0:T(8,128)S(1)}, s32[40,1024]{1,0:T(8,128)}, u32[]{:S(2)}) copy-start(s32[40,1024]{1,0:T(8,128)} %dcol_hbm.1) | copy-start | bytes 491524
  6.7 0.7 %copy-start.6 = (s32[16]{0:T(128)S(1)}, s32[16]{0:T(128)}, u32[]{:S(2)}) copy-start(s32[16]{0:T(128)} %slot_ref.1) | copy-start | bytes 196

commit v2 on v1

--- a/solution.py
+++ b/solution.py
@@ -119,116 +119,33 @@
     pack_col[0] = last
     pack_col[1] = first
 
-    n_greet = (n_lat - 1) + 2 * (n_lev - 1)
-    n_greet = n_greet + jnp.where(has_up, 2, 0) + jnp.where(has_down, 2, 0)
-    pl.semaphore_wait(barrier, n_greet)
-
-    def remote(src, dst, ssem, rsem, lat, lev):
-        return pltpu.make_async_remote_copy(
-            src_ref=src, dst_ref=dst, send_sem=ssem, recv_sem=rsem,
-            device_id=(lat, lev), device_id_type=MESH,
-        )
-
-    def halo(n, src, dst, lat, lev):
-        return remote(src, dst, halo_send.at[n], halo_recv.at[n], lat, lev)
-
-    bottom, top = pl.ds(rows - 8, 8), pl.ds(0, 8)
-    flat = [
-        halo(0, pack_col.at[0], got_col.at[0], l, east),
-        halo(1, pack_col.at[1], got_col.at[1], l, west),
-    ]
-    below = [
-        halo(2, pack_row.at[0], got_row.at[0], l + 1, e),
-        halo(3, pack_col.at[0, bottom], got_corner.at[0], l + 1, east),
-        halo(4, pack_col.at[1, bottom], got_corner.at[1], l + 1, west),
-    ]
-    above = [
-        halo(5, pack_row.at[1], got_row.at[1], l - 1, e),
-        halo(6, pack_col.at[0, top], got_corner.at[2], l - 1, east),
-        halo(7, pack_col.at[1, top], got_corner.at[3], l - 1, west),
-    ]
-
-    @pl.when(has_down)
-    def _():
-        for copy in below:
-            copy.start()
-
-    @pl.when(has_up)
-    def _():
-        for copy in above:
-            copy.start()
-
-    for copy in flat:
-        copy.start()
-
-    def spread(piece, v):
-        return pltpu.roll(piece, LANES - 2 - 2 * v, 1)
-
-    def spread_east(piece, v):
-        return pltpu.roll(piece, LANES - 2 * v, 1) if v else piece
-
-    def rim(row0, size, from_west, from_east):
-        for v in range(levels):
-            ext[v, 0, row0 : row0 + size, :] = spread(from_west, v)
-            ext[v, tiles + 1, row0 : row0 + size, :] = spread_east(from_east, v)
-
-    def fill_rows(which, row0):
-        for v in range(levels):
-            for t in range(tiles):
-                cols = slice(t * LANES, (t + 1) * LANES)
-                ext[v, t + 1, row0 : row0 + 2, :] = got_row[which, 2 * v : 2 * v + 2, cols]
-
-    @pl.when(has_up)
-    def _():
-        for copy in below:
-            copy.wait_recv()
-        fill_rows(0, 6)
-        rim(0, 8, got_corner[0], got_corner[1])
-
-    @pl.when(jnp.logical_not(has_up))
-    def _():
-        ext[:, :, 0:8, :] = jnp.zeros((levels, tiles + 2, 8, LANES), F32)
-
-    @pl.when(has_down)
-    def _():
-        for copy in above:
-            copy.wait_recv()
-        fill_rows(1, rows + 8)
-        rim(rows + 8, 8, got_corner[2], got_corner[3])
-
-    @pl.when(jnp.logical_not(has_down))
-    def _():
-        ext[:, :, rows + 8 : rows + 16, :] = jnp.zeros((levels, tiles + 2, 8, LANES), F32)
-
-    for copy in flat:
-        copy.wait_recv()
-    rim(8, rows, got_col[0], got_col[1])
-
-    tall = rows + 16
-    tall_lane = lax.broadcasted_iota(jnp.int32, (tall, LANES), 1)
-
-    def shift_tile(n, carry):
-        v, t = n // tiles, n % tiles
-        left, here, right = ext[v, t], ext[v, t + 1], ext[v, t + 2]
+    def shift_block(v, t, row0, size):
+        at = pl.ds(row0, size)
+        at_lane = lax.broadcasted_iota(jnp.int32, (size, LANES), 1)
+        left, here, right = ext[v, t, at, :], ext[v, t + 1, at, :], ext[v, t + 2, at, :]
         for n_move, move in enumerate((-2, -1, 1, 2)):
             amount = (-move) % LANES
             mine = pltpu.roll(here, amount, 1)
             if move < 0:
-                moved = jnp.where(tall_lane < -move, pltpu.roll(left, amount, 1), mine)
+                moved = jnp.where(at_lane < -move, pltpu.roll(left, amount, 1), mine)
             else:
-                moved = jnp.where(tall_lane >= LANES - move, pltpu.roll(right, amount, 1), mine)
-            shifted[n_move, v, t] = moved
-        return carry
-
-    lax.fori_loop(0, levels * tiles, shift_tile, 0)
-
-    for n in range(tiles, tiles + 3):
-        loads[n].wait()
-
-    def advect_tile(t, carry):
+                moved = jnp.where(at_lane >= LANES - move, pltpu.roll(right, amount, 1), mine)
+            shifted[n_move, v, t, at, :] = moved
+
+    def shift_inner(chosen):
+        def step(t, carry):
+            for v in chosen:
+                shift_block(v, t, 8, rows)
+            return carry
+
+        lax.fori_loop(1, tiles - 1, step, 0)
+
+    groups = rows // 8
+
+    def advect(t, chosen):
         cols = pl.ds(pl.multiple_of(t * LANES, LANES), LANES)
         corner = [wts[ab, :, cols].astype(F32) for ab in range(4)]
-        for g in range(rows // 8):
+        for g in chosen:
             band = slice(8 * g, 8 * g + 8)
             dr, dc = drow[band, cols], dcol[band, cols]
             zero = jnp.zeros((8, LANES), F32)
@@ -262,9 +179,129 @@
                         term = coef[r][c] * value
                         total = term if total is None else total + term
                 adv[v * rows + 8 * g : v * rows + 8 * g + 8, cols] = total
+
+    def advect_inner(t, carry):
+        advect(t, range(1, groups - 1))
         return carry
 
-    lax.fori_loop(0, tiles, advect_tile, 0)
+    shift_inner(range(levels // 2))
+
+    n_greet = (n_lat - 1) + 2 * (n_lev - 1)
+    n_greet = n_greet + jnp.where(has_up, 2, 0) + jnp.where(has_down, 2, 0)
+    pl.semaphore_wait(barrier, n_greet)
+
+    def remote(src, dst, ssem, rsem, lat, lev):
+        return pltpu.make_async_remote_copy(
+            src_ref=src, dst_ref=dst, send_sem=ssem, recv_sem=rsem,
+            device_id=(lat, lev), device_id_type=MESH,
+        )
+
+    def halo(n, src, dst, lat, lev):
+        return remote(src, dst, halo_send.at[n], halo_recv.at[n], lat, lev)
+
+    bottom, top = pl.ds(rows - 8, 8), pl.ds(0, 8)
+    flat = [
+        halo(0, pack_col.at[0], got_col.at[0], l, east),
+        halo(1, pack_col.at[1], got_col.at[1], l, west),
+    ]
+    below = [
+        halo(2, pack_row.at[0], got_row.at[0], l + 1, e),
+        halo(3, pack_col.at[0, bottom], got_corner.at[0], l + 1, east),
+        halo(4, pack_col.at[1, bottom], got_corner.at[1], l + 1, west),
+    ]
+    above = [
+        halo(5, pack_row.at[1], got_row.at[1], l - 1, e),
+        halo(6, pack_col.at[0, top], got_corner.at[2], l - 1, east),
+        halo(7, pack_col.at[1, top], got_corner.at[3], l - 1, west),
+    ]
+
+    @pl.when(has_down)
+    def _():
+        for copy in below:
+            copy.start()
+
+    @pl.when(has_up)
+    def _():
+        for copy in above:
+            copy.start()
+
+    for copy in flat:
+        copy.start()
+
+    shift_inner(range(levels // 2, levels))
+    for n in range(tiles, tiles + 3):
+        loads[n].wait()
+    lax.fori_loop(1, tiles - 1, advect_inner, 0)
+
+    def spread(piece, v):
+        return pltpu.roll(piece, LANES - 2 - 2 * v, 1)
+
+    def spread_east(piece, v):
+        return pltpu.roll(piece, LANES - 2 * v, 1) if v else piece
+
+    def rim(row0, size, from_west, from_east):
+        for v in range(levels):
+            ext[v, 0, row0 : row0 + size, :] = spread(from_west, v)
+            ext[v, tiles + 1, row0 : row0 + size, :] = spread_east(from_east, v)
+
+    def fill_rows(which, row0):
+        for v in range(levels):
+            for t in range(tiles):
+                cols = slice(t * LANES, (t + 1) * LANES)
+                ext[v, t + 1, row0 : row0 + 2, :] = got_row[which, 2 * v : 2 * v + 2, cols]
+
+    @pl.when(has_up)
+    def _():
+        for copy in below:
+            copy.wait_recv()
+        fill_rows(0, 6)
+        rim(0, 8, got_corner[0], got_corner[1])
+
+    @pl.when(jnp.logical_not(has_up))
+    def _():
+        ext[:, :, 0:8, :] = jnp.zeros((levels, tiles + 2, 8, LANES), F32)
+
+    @pl.when(has_down)
+    def _():
+        for copy in above:
+            copy.wait_recv()
+        fill_rows(1, rows + 8)
+        rim(rows + 8, 8, got_corner[2], got_corner[3])
+
+    @pl.when(jnp.logical_not(has_down))
+    def _():
+        ext[:, :, rows + 8 : rows + 16, :] = jnp.zeros((levels, tiles + 2, 8, LANES), F32)
+
+    for copy in flat:
+        copy.wait_recv()
+    rim(8, rows, got_col[0], got_col[1])
+
+    def shift_rims(t, carry):
+        for v in range(levels):
+            shift_block(v, t, 0, 8)
+            shift_block(v, t, rows + 8, 8)
+        return carry
+
+    def shift_edge(n, carry):
+        for v in range(levels):
+            shift_block(v, n * (tiles - 1), 8, rows)
+        return carry
+
+    edges = min(tiles, 2)
+    lax.fori_loop(0, edges, shift_edge, 0)
+    lax.fori_loop(0, tiles, shift_rims, 0)
+    outer = sorted({0, groups - 1})
+
+    def advect_rims(t, carry):
+        advect(t, outer)
+        return carry
+
+    def advect_edge(n, carry):
+        advect(n * (tiles - 1), range(groups))
+        return carry
+
+    lax.fori_loop(0, edges, advect_edge, 0)
+    lax.fori_loop(1, tiles - 1, advect_rims, 0)
 
     loads[tiles + 3].wait()
     contract_last = (((1,), (1,)), ((), ()))
@@ -322,8 +359,9 @@
         sums[1, ks, :] = imag * forward_scale
     for s in range(waves):
         k = inv[s]
-        send_s[s, 0:1, :] = sums[0, pl.ds(k, 1), :]
-        send_s[s, 1:2, :] = sums[1, pl.ds(k, 1), :]
+        chg_slot[s, 0:1, :] = sums[0, pl.ds(k, 1), :]
+        chg_slot[s, 1:2, :] = sums[1, pl.ds(k, 1), :]
+    send_s[...] = chg_slot[...].astype(BF16)
     own = waves // n_lat
     copies_s = []
     for d in others(l, n_lat):
@@ -341,9 +379,9 @@
     column = lax.broadcasted_iota(jnp.int32, (2, steps), 1)
     for p in range(2):
         start = p * (n_lat // 2)
-        raw = got_s[start]
+        raw = got_s[start].astype(F32)
         for d in range(start + 1, start + n_lat // 2):
-            raw = raw + got_s[d]
+            raw = raw + got_s[d].astype(F32)
         for so in range(own):
             wave = inv[l * own + so] * (NT + 1) // waves
             degree = wave + 2 * column + p
@@ -457,7 +495,7 @@
         own = waves // n_lat
         table = jnp.asarray(lon_table(waves))
         vmem, dma = pltpu.VMEM, pltpu.SemaphoreType.DMA
-        anywhere = pl.BlockSpec(memory_space=pl.ANY)
+        anywhere = pl.BlockSpec(memory_space=pltpu.HBM)
         in_vmem = pl.BlockSpec(memory_space=pltpu.VMEM)
         return pl.pallas_call(
             functools.partial(kernel, n_lat, n_lev),
@@ -487,8 +525,8 @@
                 vmem((waves, LANES), BF16),
                 vmem((waves, LANES), BF16),
                 vmem((2, waves, steps), F32),
-                vmem((waves, 2, steps), F32),
-                vmem((n_lat, own, 2, steps), F32),
+                vmem((waves, 2, steps), BF16),
+                vmem((n_lat, own, 2, steps), BF16),
                 vmem((2, own, 2, steps), BF16),
                 vmem((n_lat, own, 2, steps), BF16),
                 vmem((waves, 2, steps), F32),
@@ -504,7 +542,7 @@
                 dma((2, n_lev)), dma((2, n_lev)),
             ],
             compiler_params=pltpu.CompilerParams(
-                collective_id=0, has_side_effects=True, vmem_limit_bytes=48 << 20
+                collective_id=0, has_side_effects=True, vmem_limit_bytes=63 << 20
             ),
         )(wave_slot, field, weights, depart_row, depart_col, legendre, table)
 

time: 48.7 us -> 40.2 us (0.83)
  local copies, waits for them, and re-layouts: 8.17 us -> 2.6 us
  Pallas kernels: 39.6 us -> 36.8 us
    unnamed x16 -> x4, local copies, waits for them, and re-layouts: 8.17 us -> 2.6 us
    pallas_call x1, Pallas kernels: 39.6 us -> 36.8 us  [on_device(): pl.pallas_call(functools.partial(kernel, n_lat, n_lev), out_shape=(jax.Sh...]
where the time goes in v2:
time: 40.2 us; the launch traced here: 40.1 us
  Pallas kernels  36.8 us (92%)
  local copies, waits for them, and re-layouts  2.6 us (6%)
  between operations  0.65 us (2%)
    pallas_call x1, Pallas kernels, on_device(): pl.pallas_call(functools.partial(kernel, n_lat, n_lev), out_shape=(jax.Sh...  36.8 us
    unnamed x4, local copies, waits for them, and re-layouts  2.6 us

profile of v2, /device:TPU:0, one launch (start us, length us, event | category | flops | bytes accessed | tf_op | source)
XLA Modules:
  0.0 40.1 jit_solution(18115642077429278704)
XLA Ops:
  0.6 36.8 %shard_map.86 = (f32[4,40,1024]{2,1,0:T(8,128)}, f32[2,2,1,2,640]{4,3,2,1,0:T(2,128)}) custom-call(s32[16]{0:T(128)} %slot_ref.1, f32[4,40,1024]{2,1,0:T(8,128)} %field_hbm.1, bf16[4,40,1024]{2,1,0:T(8,128)(2,1)} %weights_hbm.1, s32[40,1024]{1,0:T(8,128)} %drow_hbm.1, s32[40,1024]{1,0:T(8,128)} %dcol_hbm.1, bf16[40,16,640]{2,1,0:T(8,128)(2,1)} %leg_hbm.1, ...), custom_call_target="tpu_custom_call" | custom-call | tf_op jit(solution)/shard_map/pallas_call | solution.py:500
  37.5 0.0 copy-start
  37.5 2.0 %copy.11 = f32[4,40,1024]{2,1,0:T(8,128)} copy(f32[4,40,1024]{2,1,0:T(8,128)} %get-tuple-element.4) | data formatting | bytes 1310720
  39.5 0.0 copy-done
  39.5 0.6 %copy.12 = f32[2,2,1,2,640]{4,3,2,1,0:T(2,128)} copy(f32[2,2,1,2,640]{4,3,2,1,0:T(2,128)S(1)} %copy-done) | data formatting | bytes 40960
Async XLA Ops:
  37.5 2.0 %copy-start = (f32[2,2,1,2,640]{4,3,2,1,0:T(2,128)S(1)}, f32[2,2,1,2,640]{4,3,2,1,0:T(2,128)}, u32[]{:S(2)}) copy-start(f32[2,2,1,2,640]{4,3,2,1,0:T(2,128)} %get-tuple-element.5) | copy-start | bytes 61444

commit v3 on v2

--- a/solution.py
+++ b/solution.py
@@ -88,15 +88,6 @@
     def _():
         greet(l + 1, east)
         greet(l + 1, west)
-
-    def find(s, carry):
-        def step(k, found):
-            return jnp.where(slot_ref[k] == s, k, found)
-
-        inv[s] = lax.fori_loop(0, waves, step, jnp.int32(0))
-        return carry
-
-    lax.fori_loop(0, waves, find, 0)
 
     lane = lax.broadcasted_iota(jnp.int32, (rows, LANES), 1)
     for t in range(tiles):
@@ -119,11 +110,14 @@
     pack_col[0] = last
     pack_col[1] = first
 
-    def shift_block(v, t, row0, size):
+    def shift_block(v, t, row0, size, moves=(-2, -1, 1, 2)):
         at = pl.ds(row0, size)
         at_lane = lax.broadcasted_iota(jnp.int32, (size, LANES), 1)
-        left, here, right = ext[v, t, at, :], ext[v, t + 1, at, :], ext[v, t + 2, at, :]
-        for n_move, move in enumerate((-2, -1, 1, 2)):
+        here = ext[v, t + 1, at, :]
+        left = ext[v, t, at, :] if min(moves) < 0 else None
+        right = ext[v, t + 2, at, :] if max(moves) > 0 else None
+        for move in moves:
+            n_move = (-2, -1, 1, 2).index(move)
             amount = (-move) % LANES
             mine = pltpu.roll(here, amount, 1)
             if move < 0:
@@ -228,7 +222,20 @@
     for copy in flat:
         copy.start()
 
+    def find(s, carry):
+        def step(k, found):
+            return jnp.where(slot_ref[k] == s, k, found)
+
+        inv[s] = lax.fori_loop(0, waves, step, jnp.int32(0))
+        return carry
+
+    lax.fori_loop(0, waves, find, 0)
+
     shift_inner(range(levels // 2, levels))
+    if tiles > 1:
+        for v in range(levels):
+            shift_block(v, 0, 8, rows, (1, 2))
+            shift_block(v, tiles - 1, 8, rows, (-2, -1))
     for n in range(tiles, tiles + 3):
         loads[n].wait()
     lax.fori_loop(1, tiles - 1, advect_inner, 0)
@@ -282,13 +289,10 @@
             shift_block(v, t, rows + 8, 8)
         return carry
 
-    def shift_edge(n, carry):
-        for v in range(levels):
-            shift_block(v, n * (tiles - 1), 8, rows)
-        return carry
-
     edges = min(tiles, 2)
-    lax.fori_loop(0, edges, shift_edge, 0)
+    for v in range(levels):
+        shift_block(v, 0, 8, rows, (-2, -1))
+        shift_block(v, tiles - 1, 8, rows, (1, 2))
     lax.fori_loop(0, tiles, shift_rims, 0)
     outer = sorted({0, groups - 1})
 
@@ -361,7 +365,7 @@
         k = inv[s]
         chg_slot[s, 0:1, :] = sums[0, pl.ds(k, 1), :]
         chg_slot[s, 1:2, :] = sums[1, pl.ds(k, 1), :]
-    send_s[...] = chg_slot[...].astype(BF16)
+    send_s[...] = chg_slot[...]
     own = waves // n_lat
     copies_s = []
     for d in others(l, n_lat):
@@ -379,9 +383,9 @@
     column = lax.broadcasted_iota(jnp.int32, (2, steps), 1)
     for p in range(2):
         start = p * (n_lat // 2)
-        raw = got_s[start].astype(F32)
+        raw = got_s[start]
         for d in range(start + 1, start + n_lat // 2):
-            raw = raw + got_s[d].astype(F32)
+            raw = raw + got_s[d]
         for so in range(own):
             wave = inv[l * own + so] * (NT + 1) // waves
             degree = wave + 2 * column + p
@@ -525,8 +529,8 @@
                 vmem((waves, LANES), BF16),
                 vmem((waves, LANES), BF16),
                 vmem((2, waves, steps), F32),
-                vmem((waves, 2, steps), BF16),
-                vmem((n_lat, own, 2, steps), BF16),
+                vmem((waves, 2, steps), F32),
+                vmem((n_lat, own, 2, steps), F32),
                 vmem((2, own, 2, steps), BF16),
                 vmem((n_lat, own, 2, steps), BF16),
                 vmem((waves, 2, steps), F32),
@@ -542,7 +546,7 @@
                 dma((2, n_lev)), dma((2, n_lev)),
             ],
             compiler_params=pltpu.CompilerParams(
-                collective_id=0, has_side_effects=True, vmem_limit_bytes=63 << 20
+                collective_id=0, has_side_effects=True, vmem_limit_bytes=32 << 20
             ),
         )(wave_slot, field, weights, depart_row, depart_col, legendre, table)
 

time: 40.2 us -> 45.2 us (1.12)
  local copies, waits for them, and re-layouts: 2.6 us -> 8.17 us
  Pallas kernels: 36.8 us -> 36 us
    unnamed x4 -> x16, local copies, waits for them, and re-layouts: 2.6 us -> 8.17 us
    pallas_call x1, Pallas kernels: 36.8 us -> 36 us  [on_device(): pl.pallas_call(functools.partial(kernel, n_lat, n_lev), out_shape=(jax.Sh...]
where the time goes in v3:
time: 45.2 us; the launch traced here: 44.8 us
  Pallas kernels  36 us (80%)
  local copies, waits for them, and re-layouts  8.17 us (18%)
  between operations  0.65 us (1%)
    pallas_call x1, Pallas kernels, on_device(): pl.pallas_call(functools.partial(kernel, n_lat, n_lev), out_shape=(jax.Sh...  36 us
    unnamed x16, local copies, waits for them, and re-layouts  8.17 us

profile of v3, /device:TPU:0, one launch (start us, length us, event | category | flops | bytes accessed | tf_op | source)
XLA Modules:
  0.0 44.8 jit_solution(11945050007707036497)
XLA Ops:
  0.6 0.0 copy-start
  0.6 1.1 %copy-done = bf16[40,16,640]{2,1,0:T(8,128)(2,1)S(1)} copy-done((bf16[40,16,640]{2,1,0:T(8,128)(2,1)S(1)}, bf16[40,16,640]{2,1,0:T(8,128)(2,1)}, u32[]{:S(2)}) %copy-start) | copy-done | bytes 819224
  1.8 0.0 copy-start.1
  1.8 1.1 %copy-done.1 = f32[4,40,1024]{2,1,0:T(8,128)S(1)} copy-done((f32[4,40,1024]{2,1,0:T(8,128)S(1)}, f32[4,40,1024]{2,1,0:T(8,128)}, u32[]{:S(2)}) %copy-start.1) | copy-done | bytes 655384
  2.9 0.0 copy-start.2
  2.9 1.0 %copy-done.2 = bf16[64,4096]{1,0:T(8,128)(2,1)S(1)} copy-done((bf16[64,4096]{1,0:T(8,128)(2,1)S(1)}, bf16[64,4096]{1,0:T(8,128)(2,1)}, u32[]{:S(2)}) %copy-start.2) | copy-done | bytes 524312
  3.9 0.0 copy-start.3
  3.9 1.0 %copy-done.3 = bf16[4,40,1024]{2,1,0:T(8,128)(2,1)S(1)} copy-done((bf16[4,40,1024]{2,1,0:T(8,128)(2,1)S(1)}, bf16[4,40,1024]{2,1,0:T(8,128)(2,1)}, u32[]{:S(2)}) %copy-start.3) | copy-done | bytes 327704
  4.9 0.0 copy-start.4
  4.9 0.9 %copy-done.4 = s32[40,1024]{1,0:T(8,128)S(1)} copy-done((s32[40,1024]{1,0:T(8,128)S(1)}, s32[40,1024]{1,0:T(8,128)}, u32[]{:S(2)}) %copy-start.4) | copy-done | bytes 163864
  5.8 0.0 copy-start.5
  5.8 0.9 %copy-done.5 = s32[40,1024]{1,0:T(8,128)S(1)} copy-done((s32[40,1024]{1,0:T(8,128)S(1)}, s32[40,1024]{1,0:T(8,128)}, u32[]{:S(2)}) %copy-start.5) | copy-done | bytes 163864
  6.7 0.0 copy-start.6
  6.7 0.7 %copy-done.6 = s32[16]{0:T(128)S(1)} copy-done((s32[16]{0:T(128)S(1)}, s32[16]{0:T(128)}, u32[]{:S(2)}) %copy-start.6) | copy-done | bytes 88
  7.4 36.0 %shard_map.86 = (f32[4,40,1024]{2,1,0:T(8,128)S(1)}, f32[2,2,1,2,640]{4,3,2,1,0:T(2,128)S(1)}) custom-call(s32[16]{0:T(128)S(1)} %copy-done.6, f32[4,40,1024]{2,1,0:T(8,128)S(1)} %copy-done.1, bf16[4,40,1024]{2,1,0:T(8,128)(2,1)S(1)} %copy-done.3, s32[40,1024]{1,0:T(8,128)S(1)} %copy-done.4, s32[40,1024]{1,0:T(8,128)S(1)} %copy-done.5, ...), custom_call_target="tpu_custom_call" | custom-call | tf_op jit(solution)/shard_map/pallas_call | solution.py:504
  43.4 0.8 %copy.11 = f32[4,40,1024]{2,1,0:T(8,128)} copy(f32[4,40,1024]{2,1,0:T(8,128)S(1)} %get-tuple-element.4) | data formatting | bytes 1310720
  44.2 0.6 %copy.12 = f32[2,2,1,2,640]{4,3,2,1,0:T(2,128)} copy(f32[2,2,1,2,640]{4,3,2,1,0:T(2,128)S(1)} %get-tuple-element.5) | data formatting | bytes 40960
Async XLA Ops:
  0.6 1.1 %copy-start = (bf16[40,16,640]{2,1,0:T(8,128)(2,1)S(1)}, bf16[40,16,640]{2,1,0:T(8,128)(2,1)}, u32[]{:S(2)}) copy-start(bf16[40,16,640]{2,1,0:T(8,128)(2,1)} %leg_hbm.1) | copy-start | bytes 2457604
  1.8 1.1 %copy-start.1 = (f32[4,40,1024]{2,1,0:T(8,128)S(1)}, f32[4,40,1024]{2,1,0:T(8,128)}, u32[]{:S(2)}) copy-start(f32[4,40,1024]{2,1,0:T(8,128)} %field_hbm.1) | copy-start | bytes 1966084
  2.9 1.0 %copy-start.2 = (bf16[64,4096]{1,0:T(8,128)(2,1)S(1)}, bf16[64,4096]{1,0:T(8,128)(2,1)}, u32[]{:S(2)}) copy-start(bf16[64,4096]{1,0:T(8,128)(2,1)} %constant.2.clone.table_hbm) | copy-start | bytes 1572868
  3.9 1.0 %copy-start.3 = (bf16[4,40,1024]{2,1,0:T(8,128)(2,1)S(1)}, bf16[4,40,1024]{2,1,0:T(8,128)(2,1)}, u32[]{:S(2)}) copy-start(bf16[4,40,1024]{2,1,0:T(8,128)(2,1)} %weights_hbm.1) | copy-start | bytes 983044
  4.9 0.9 %copy-start.4 = (s32[40,1024]{1,0:T(8,128)S(1)}, s32[40,1024]{1,0:T(8,128)}, u32[]{:S(2)}) copy-start(s32[40,1024]{1,0:T(8,128)} %drow_hbm.1) | copy-start | bytes 491524
  5.8 0.9 %copy-start.5 = (s32[40,1024]{1,0:T(8,128)S(1)}, s32[40,1024]{1,0:T(8,128)}, u32[]{:S(2)}) copy-start(s32[40,1024]{1,0:T(8,128)} %dcol_hbm.1) | copy-start | bytes 491524
  6.7 0.7 %copy-start.6 = (s32[16]{0:T(128)S(1)}, s32[16]{0:T(128)}, u32[]{:S(2)}) copy-start(s32[16]{0:T(128)} %slot_ref.1) | copy-start | bytes 196

commit v4 on v3

--- a/solution.py
+++ b/solution.py
@@ -33,12 +33,12 @@
 def kernel(
     n_lat, n_lev,
     slot_ref, field_hbm, weights_hbm, drow_hbm, dcol_hbm, leg_hbm, table_hbm,
-    out_ref, spec_ref,
+    out_ref, spec_ref, adv_hbm,
     ext, shifted, wts, drow, dcol, leg, tab, adv, inv,
     pack_row, pack_col, got_row, got_col, got_corner,
     send_f, got_f, send_x, got_x, sums, send_s, got_s, send_c, got_c,
     chg_slot, chg, send_h, got_h,
-    load_sem, halo_send, halo_recv, f_send, f_recv, x_send, x_recv,
+    load_sem, adv_sem, halo_send, halo_recv, f_send, f_recv, x_send, x_recv,
     s_send, s_recv, c_send, c_recv, h_send, h_recv,
 ):
     levels, rows, width = out_ref.shape
@@ -306,6 +306,14 @@
 
     lax.fori_loop(0, edges, advect_edge, 0)
     lax.fori_loop(1, tiles - 1, advect_rims, 0)
+
+    copies_adv = []
+    for v in range(levels):
+        copy = pltpu.make_async_copy(
+            adv.at[pl.ds(v * rows, rows), :], adv_hbm.at[v], adv_sem.at[v]
+        )
+        copy.start()
+        copies_adv.append(copy)
 
     loads[tiles + 3].wait()
     contract_last = (((1,), (1,)), ((), ()))
@@ -471,10 +479,11 @@
             + jnp.dot(lead, table_rest, preferred_element_type=F32)
             + jnp.dot(rest, table, preferred_element_type=F32)
         )
-        updated = adv[:, cols] + increment
         for v in range(levels):
-            out_ref[v, :, cols] = updated[v * rows : (v + 1) * rows]
-
+            out_ref[v, :, cols] = increment[v * rows : (v + 1) * rows]
+
+    for copy in copies_adv:
+        copy.wait()
     for copy in flat + copies_f + [copy_x] + copies_s + copies_c + copies_h:
         copy.wait_send()
 
@@ -501,14 +510,15 @@
         vmem, dma = pltpu.VMEM, pltpu.SemaphoreType.DMA
         anywhere = pl.BlockSpec(memory_space=pltpu.HBM)
         in_vmem = pl.BlockSpec(memory_space=pltpu.VMEM)
-        return pl.pallas_call(
+        increment, spectral, advected = pl.pallas_call(
             functools.partial(kernel, n_lat, n_lev),
             out_shape=(
                 jax.ShapeDtypeStruct((levels, rows, width), F32),
                 jax.ShapeDtypeStruct((own, 2, 1, 2, steps), F32),
+                jax.ShapeDtypeStruct((levels, rows, width), F32),
             ),
             in_specs=[pl.BlockSpec(memory_space=pltpu.SMEM)] + [anywhere] * 6,
-            out_specs=(in_vmem, in_vmem),
+            out_specs=(in_vmem, in_vmem, anywhere),
             scratch_shapes=[
                 vmem((levels, tiles + 2, rows + 16, LANES), F32),
                 vmem((4, levels, tiles, rows + 16, LANES), F32),
@@ -537,7 +547,7 @@
                 vmem((2, waves, steps), F32),
                 vmem((2, waves, LANES), F32),
                 vmem((2, n_lev, waves, LANES), F32),
-                dma((tiles + 5,)),
+                dma((tiles + 5,)), dma((levels,)),
                 dma((8,)), dma((8,)),
                 dma((n_lev,)), dma((n_lev,)),
                 dma, dma,
@@ -546,9 +556,10 @@
                 dma((2, n_lev)), dma((2, n_lev)),
             ],
             compiler_params=pltpu.CompilerParams(
-                collective_id=0, has_side_effects=True, vmem_limit_bytes=32 << 20
+                collective_id=0, has_side_effects=True, vmem_limit_bytes=63 << 20
             ),
         )(wave_slot, field, weights, depart_row, depart_col, legendre, table)
+        return (advected + increment, spectral)
 
     placed = (
         P(None, "lat", "lev"),

time: 45.2 us -> 40.1 us (0.89)
  local copies, waits for them, and re-layouts: 8.17 us -> 0.61 us
  other arithmetic: 0 us -> 2.22 us
    unnamed x16 -> x3, local copies, waits for them, and re-layouts: 8.17 us -> 0.61 us
    add x0 -> x1, other arithmetic: none -> 2.22 us  [on_device(): return (advected + increment, spectral)]
where the time goes in v4:
time: 40.1 us; the launch traced here: 39.9 us
  Pallas kernels  36.4 us (91%)
  other arithmetic  2.22 us (6%)
  between operations  0.65 us (2%)
  local copies, waits for them, and re-layouts  0.61 us (2%)
    pallas_call x1, Pallas kernels, on_device(): pl.pallas_call(functools.partial(kernel, n_lat, n_lev), out_shape=(jax.Sh...  36.4 us
    add x1, other arithmetic, on_device(): return (advected + increment, spectral)  2.22 us

profile of v4, /device:TPU:0, one launch (start us, length us, event | category | flops | bytes accessed | tf_op | source)
XLA Modules:
  0.0 39.9 jit_solution(7440830516604471312)
XLA Ops:
  0.6 36.4 %shard_map.86 = (f32[4,40,1024]{2,1,0:T(8,128)}, f32[2,2,1,2,640]{4,3,2,1,0:T(2,128)}, f32[4,40,1024]{2,1,0:T(8,128)}) custom-call(s32[16]{0:T(128)} %slot_ref.1, f32[4,40,1024]{2,1,0:T(8,128)} %field_hbm.1, bf16[4,40,1024]{2,1,0:T(8,128)(2,1)} %weights_hbm.1, s32[40,1024]{1,0:T(8,128)} %drow_hbm.1, s32[40,1024]{1,0:T(8,128)} %dcol_hbm.1, ...), custom_call_target="tpu_custom_call" | custom-call | tf_op jit(solution)/shard_map/pallas_call | solution.py:513
  37.1 0.0 copy-start
  37.1 2.2 %add.3 = f32[4,40,1024]{2,1,0:T(8,128)} add(f32[4,40,1024]{2,1,0:T(8,128)} %get-tuple-element.5, f32[4,40,1024]{2,1,0:T(8,128)} %get-tuple-element.6) | non-fusion elementwise | flops 163840 | bytes 1966080 | tf_op jit(solution)/shard_map/add | solution.py:562
  39.3 0.0 copy-done
  39.3 0.6 %copy.10 = f32[2,2,1,2,640]{4,3,2,1,0:T(2,128)} copy(f32[2,2,1,2,640]{4,3,2,1,0:T(2,128)S(1)} %copy-done) | data formatting | bytes 40960
Async XLA Ops:
  37.1 2.2 %copy-start = (f32[2,2,1,2,640]{4,3,2,1,0:T(2,128)S(1)}, f32[2,2,1,2,640]{4,3,2,1,0:T(2,128)}, u32[]{:S(2)}) copy-start(f32[2,2,1,2,640]{4,3,2,1,0:T(2,128)} %get-tuple-element.11) | copy-start | bytes 61444

commit v5 on v3

--- a/solution.py
+++ b/solution.py
@@ -546,7 +546,7 @@
                 dma((2, n_lev)), dma((2, n_lev)),
             ],
             compiler_params=pltpu.CompilerParams(
-                collective_id=0, has_side_effects=True, vmem_limit_bytes=32 << 20
+                collective_id=0, has_side_effects=True, vmem_limit_bytes=63 << 20
             ),
         )(wave_slot, field, weights, depart_row, depart_col, legendre, table)
 

time: 45.2 us -> 39.8 us (0.88)
  local copies, waits for them, and re-layouts: 8.17 us -> 2.6 us
    unnamed x16 -> x4, local copies, waits for them, and re-layouts: 8.17 us -> 2.6 us
where the time goes in v5:
time: 39.8 us; the launch traced here: 39.6 us
  Pallas kernels  36.4 us (91%)
  local copies, waits for them, and re-layouts  2.6 us (7%)
  between operations  0.65 us (2%)
    pallas_call x1, Pallas kernels, on_device(): pl.pallas_call(functools.partial(kernel, n_lat, n_lev), out_shape=(jax.Sh...  36.4 us
    unnamed x4, local copies, waits for them, and re-layouts  2.6 us

profile of v5, /device:TPU:0, one launch (start us, length us, event | category | flops | bytes accessed | tf_op | source)
XLA Modules:
  0.0 39.6 jit_solution(9359505329240801094)
XLA Ops:
  0.6 36.4 %shard_map.86 = (f32[4,40,1024]{2,1,0:T(8,128)}, f32[2,2,1,2,640]{4,3,2,1,0:T(2,128)}) custom-call(s32[16]{0:T(128)} %slot_ref.1, f32[4,40,1024]{2,1,0:T(8,128)} %field_hbm.1, bf16[4,40,1024]{2,1,0:T(8,128)(2,1)} %weights_hbm.1, s32[40,1024]{1,0:T(8,128)} %drow_hbm.1, s32[40,1024]{1,0:T(8,128)} %dcol_hbm.1, bf16[40,16,640]{2,1,0:T(8,128)(2,1)} %leg_hbm.1, ...), custom_call_target="tpu_custom_call" | custom-call | tf_op jit(solution)/shard_map/pallas_call | solution.py:504
  37.0 0.0 copy-start
  37.0 2.0 %copy.11 = f32[4,40,1024]{2,1,0:T(8,128)} copy(f32[4,40,1024]{2,1,0:T(8,128)} %get-tuple-element.4) | data formatting | bytes 1310720
  39.0 0.0 copy-done
  39.0 0.6 %copy.12 = f32[2,2,1,2,640]{4,3,2,1,0:T(2,128)} copy(f32[2,2,1,2,640]{4,3,2,1,0:T(2,128)S(1)} %copy-done) | data formatting | bytes 40960
Async XLA Ops:
  37.0 2.0 %copy-start = (f32[2,2,1,2,640]{4,3,2,1,0:T(2,128)S(1)}, f32[2,2,1,2,640]{4,3,2,1,0:T(2,128)}, u32[]{:S(2)}) copy-start(f32[2,2,1,2,640]{4,3,2,1,0:T(2,128)} %get-tuple-element.5) | copy-start | bytes 61444
